TPU v7x, 32 devices: a whole 2x2x4 slice. The times are simulated.
32 devices in a mesh: fsdp: 2 (over y), tensor: 4 (over x, core), replica: 4 (over z).
Axes of the slice: x: 2, y: 2, z: 4, core: 2. Of those that a mesh axis runs over, the one named last changes fastest.
Arguments:
- gradient: bfloat16 [4, 4096, 8192], P('replica', 'fsdp', 'tensor'), may hold values from -400 to 400, as said below
- momentum: float32 [4, 4096, 8192], P('replica', 'fsdp', 'tensor'), may hold values from -6 to 6
- basis: float32 [8192, 256], P('tensor', 'fsdp'), may hold values from -0.0625 to 0.0625
Outputs:
- update: bfloat16 [4096, 8192], P('fsdp', 'tensor')
- momentum_new: float32 [4, 4096, 8192], P('replica', 'fsdp', 'tensor')
- basis_new: float32 [8192, 256], P('tensor', 'fsdp')
Inputs may be any that keep to these rules, and one draw needn't show every extreme that they name: gradient entries are finite real numbers.
All inputs are finite; a program needn't handle non-finite values.
Results may differ from a plain program's by a relative error of at most 0.001.
Values sent between devices are 32-bit elements; how exact they have to be, the bound alone decides.
A program may use at most 128 MiB of HBM per device.

v0:
```python
import jax
import jax.numpy as jnp
from jax import lax
from jax.sharding import PartitionSpec as P

M_ROWS = 4096
NCOLS = 8192
RANK = 256
HIGH = lax.Precision.HIGHEST


def local(gradient, momentum, basis):
    replicas = lax.axis_size("replica")
    rank_local = basis.shape[1]
    buffer = momentum[0] + gradient[0].astype(jnp.float32)
    partial_value = jnp.dot(
        buffer,
        lax.all_gather(basis, "fsdp", axis=1, tiled=True),
        precision=HIGH,
        preferred_element_type=jnp.float32,
    )
    left = lax.psum(partial_value, ("tensor", "replica")) / replicas
    local_gram = jnp.dot(left.T, left, precision=HIGH, preferred_element_type=jnp.float32)
    gram = lax.psum(local_gram, "fsdp")
    chol = jnp.linalg.cholesky(gram)
    ortho = lax.linalg.triangular_solve(chol, left, left_side=False, lower=True, transpose_a=True)
    right_part = jnp.dot(buffer.T, ortho, precision=HIGH, preferred_element_type=jnp.float32)
    right = lax.psum(right_part, ("fsdp", "replica")) / replicas
    squares = lax.psum(jnp.sum(right * right, axis=0), "tensor")
    norms = jnp.sqrt(squares + 1e-12)
    basis_full = right / norms
    lowrank = jnp.dot(ortho, right.T, precision=HIGH, preferred_element_type=jnp.float32)
    momentum_new = (buffer - 0.05 * lowrank)[None]
    scale = (M_ROWS * NCOLS / RANK) ** 0.5
    update = (
        scale * jnp.dot(ortho, basis_full.T, precision=HIGH, preferred_element_type=jnp.float32)
    ).astype(jnp.bfloat16)
    offset = lax.axis_index("fsdp") * rank_local
    basis_new = lax.dynamic_slice_in_dim(basis_full, offset, rank_local, 1)
    return (update, momentum_new, basis_new)


def solution(mesh):
    return jax.shard_map(
        local,
        mesh=mesh,
        in_specs=(
            P("replica", "fsdp", "tensor"),
            P("replica", "fsdp", "tensor"),
            P("tensor", "fsdp"),
        ),
        out_specs=(P("fsdp", "tensor"), P("replica", "fsdp", "tensor"), P("tensor", "fsdp")),
        check_vma=False,
    )
```

profile of v0, /device:TPU:0, one launch (start us, length us, event | category | flops | bytes accessed | tf_op | source)
XLA Modules:
  0.0 472.0 jit_solution(12130268575645546304)
XLA Ops:
  7.2 0.7 all-gather.2.cloned.1.call-update
  7.9 37.4 %all-gather.2.cloned.1.call-done = f32[2048,256]{1,0:T(8,128)} async-done(((f32[2048,128]{1,0:T(8,128)}), f32[2048,256]{1,0:T(8,128)}) %all-gather.2.cloned.1.call-update) | async-done | bytes 2097168 | tf_op jit(solution)/shard_map/all_gather | solution.py:18
  45.3 18.8 %fusion.2 = f32[2048,256]{1,0:T(8,128)} fusion(f32[2048,256]{1,0:T(8,128)} %all-gather.2.cloned.1.call-done, f32[1,2048,2048]{2,1,0:T(8,128)} %param.4, bf16[1,2048,2048]{2,1,0:T(8,128)(2,1)} %param.3), kind=kOutput, calls=%fused_computation.5 | convolution fusion | flops 12893290496 | bytes 29360128 | tf_op jit(solution)/shard_map/dot_general | solution.py:16
  64.3 98.4 %all-reduce.5.cloned.1.call-done = f32[2048,256]{1,0:T(8,128)} async-done(((f32[2048,256]{1,0:T(8,128)}), f32[2048,256]{1,0:T(8,128)}) %all-reduce.5.cloned.1.call-update) | async-done | bytes 2097168 | tf_op jit(solution)/shard_map/psum | solution.py:22
  162.6 6.4 %fusion.19 = f32[256,256]{0,1:T(8,128)} fusion(f32[2048,256]{1,0:T(8,128)} %all-reduce.5.cloned.1.call-done), kind=kOutput, calls=%fused_computation.47 | convolution fusion | flops 1611137024 | bytes 2359296 | tf_op jit(solution)/shard_map/dot_general | solution.py:23
  169.1 0.6 all-reduce.9.cloned.1.call-start
  169.6 1.7 broadcast_multiply_fusion
  171.4 20.4 %all-reduce.7.cloned.1.call-done = f32[256,256]{0,1:T(8,128)} async-done(((f32[256,256]{0,1:T(8,128)}), f32[256,256]{0,1:T(8,128)}) %all-reduce.7.cloned.1.call-update) | async-done | bytes 262160 | tf_op jit(solution)/shard_map/psum | solution.py:24
  191.7 1.1 copy.7
  192.8 1.0 fusion.9
  193.8 11.7 %cholesky.50 = f32[128,128]{1,0:T(8,128)S(1)} custom-call(f32[128,128]{1,0:T(8,128)S(1)} %cholesky.118), custom_call_target="Cholesky" | custom-call | tf_op jit(solution)/shard_map/jit(cholesky)/cholesky | solution.py:25
  205.6 9.8 %custom-call.14 = f32[1,128,128]{1,2,0:T(8,128)S(1)} custom-call(f32[1,128,128]{2,1,0:T(8,128)S(1)} %get-tuple-element.24), custom_call_target="InvertDiagBlocksLowerTriangular" | custom-call | tf_op jit(solution)/shard_map/jit(cholesky)/cholesky | solution.py:25
  215.9 11.7 %cholesky.105 = f32[128,128]{1,0:T(8,128)S(1)} custom-call(f32[128,128]{1,0:T(8,128)S(1)} %convolution_subtract_fusion.1), custom_call_target="Cholesky" | custom-call | tf_op jit(solution)/shard_map/jit(cholesky)/cholesky | solution.py:25
  227.6 0.6 compare_reduce_fusion
  229.7 4.2 while.1
  229.9 0.6 fusion.28
  230.5 1.4 bitcast_dynamic-update-slice_fusion.2
  231.9 0.6 fusion.28
  232.5 1.4 bitcast_dynamic-update-slice_fusion.2
  233.9 19.7 %custom-call.15 = f32[2,128,128]{1,2,0:T(8,128)S(1)} custom-call(f32[2,128,128]{2,1,0:T(8,128)S(1)} %get-tuple-element.10), custom_call_target="InvertDiagBlocksLowerTriangular" | custom-call | tf_op jit(solution)/shard_map/triangular_solve | solution.py:26
  253.5 1.1 fusion.6
  254.6 1.8 convolution_subtract_fusion
  256.5 1.1 fusion.10
  257.6 1.0 copy-done.1
  258.5 31.3 %fusion = f32[2048,256]{1,0:T(8,128)} fusion(f32[1,2048,2048]{2,1,0:T(8,128)} %param.4, bf16[1,2048,2048]{2,1,0:T(8,128)(2,1)} %param.3, f32[2048,128]{0,1:T(8,128)S(1)} %fusion.10, f32[2048,128]{0,1:T(8,128)S(1)} %fusion.6), kind=kOutput, calls=%fused_computation.3 | convolution fusion | flops 12893814784 | bytes 29360128 | tf_op jit(solution)/shard_map/dot_general | solution.py:27
  289.8 102.4 %all-reduce.9.cloned.1.call-done = f32[2048,256]{1,0:T(8,128)} async-done(((f32[2048,256]{1,0:T(8,128)}), f32[2048,256]{1,0:T(8,128)}) %all-reduce.9.cloned.1.call-update) | async-done | bytes 2097168 | tf_op jit(solution)/shard_map/psum | solution.py:28
  392.3 2.0 multiply_reduce_fusion
  394.3 6.4 %psum.31 = f32[256]{0:T(256)S(1)} all-reduce(f32[256]{0:T(256)S(1)} %multiply_reduce_fusion), channel_id=1, replica_groups=mesh['fsdp'=2,'tensor'=4,'replica'=4] {'tensor'}, use_global_device_ids=true, to_apply=%region_8.9 | all-reduce | flops 256 | bytes 2048 | tf_op jit(solution)/shard_map/psum | solution.py:29
  400.9 1.1 copy-done.2
  401.9 28.8 %multiply_convert_fusion = bf16[2048,2048]{1,0:T(8,128)(2,1)} fusion(f32[2048,256]{1,0:T(8,128)S(1)} %multiply_divide_fusion, f32[2048,128]{0,1:T(8,128)S(1)} %copy-done.2, f32[2048,128]{0,1:T(8,128)S(1)} %fusion.6), kind=kOutput, calls=%fused_computation.8 | convolution fusion | flops 12893814784 | bytes 12582912 | tf_op jit(solution)/shard_map/dot_general | solution.py:36
  430.8 1.0 constant_dynamic-slice_fusion.1
  431.8 33.1 %fusion.4 = f32[1,2048,2048]{2,1,0:T(8,128)} fusion(f32[1,2048,2048]{2,1,0:T(8,128)} %param.4, bf16[1,2048,2048]{2,1,0:T(8,128)(2,1)} %param.3, f32[2048,256]{1,0:T(8,128)S(1)} %copy-done, f32[2048,128]{0,1:T(8,128)S(1)} %copy-done.2, f32[2048,128]{0,1:T(8,128)S(1)} %fusion.6), kind=kOutput, calls=%fused_computation.7 | convolution fusion | flops 12902727680 | bytes 46137344 | tf_op jit(solution)/shard_map/dot_general | solution.py:32
  (24 shorter events, 1.0 us)
Async XLA Ops:
  7.2 38.2 %all-gather.2.cloned.1.call-start = ((), (), s32[]{:S(2)}) async-start(), calls=%async_computation | async-start | bytes 3145728 | tf_op jit(solution)/shard_map/all_gather | solution.py:18
  7.9 154.7 %all-reduce.5.cloned.1.call-start = ((), (), s32[]{:S(2)}) async-start(), calls=%async_computation.1 | async-start | bytes 4194304 | tf_op jit(solution)/shard_map/psum | solution.py:22
  64.2 127.5 %all-reduce.7.cloned.1.call-start = ((), (), s32[]{:S(2)}) async-start(), calls=%async_computation.2 | async-start | bytes 524288 | tf_op jit(solution)/shard_map/psum | solution.py:24
  169.1 223.2 %all-reduce.9.cloned.1.call-start = ((), (), s32[]{:S(2)}) async-start(), calls=%async_computation.3 | async-start | bytes 4194304 | tf_op jit(solution)/shard_map/psum | solution.py:28
  257.6 1.0 copy-start.1
  392.3 8.4 %copy-start = (f32[2048,256]{1,0:T(8,128)S(1)}, f32[2048,256]{1,0:T(8,128)}, u32[]{:S(2)}) copy-start(f32[2048,256]{1,0:T(8,128)} %all-reduce.9.cloned.1.call-done) | copy-start | bytes 6291460
  400.7 1.2 copy-start.2
Sparse Core Ops, SparseCore 0:
  9.5 35.7 all-gather.1
  64.3 98.2 all-reduce.4
  169.2 22.4 all-reduce.6
  289.9 102.2 all-reduce.8
where the time goes:
time: 478 us; the launch traced here: 472 us
  waiting for transfers between devices  259 us (54%)
  matrix products  123 us (26%)
  other arithmetic  58.6 us (12%)
  between operations  15.7 us (3%)
  local copies, waits for them, and re-layouts  8.2 us (2%)
  blocking collectives  6.38 us (1%)
    psum x1, waiting for transfers between devices, local(): right = lax.psum(right_part, ('fsdp', 'replica')) / replicas  102 us
    psum x1, waiting for transfers between devices, local(): left = lax.psum(partial_value, ('tensor', 'replica')) / replicas  98.4 us
    all_gather x1, waiting for transfers between devices, local(): lax.all_gather(basis, 'fsdp', axis=1, tiled=True)  37.4 us
    another operation x6, other arithmetic, local(): chol = jnp.linalg.cholesky(gram)  34 us
    dot_general x1, matrix products, local(): jnp.dot(ortho, right.T, precision=HIGH, preferred_element_type=jnp.float32)  33.1 us
    dot_general x1, matrix products, local(): jnp.dot(buffer.T, ortho, precision=HIGH, preferred_element_type=jnp.float32)  31.3 us
    dot_general x1, matrix products, local(): jnp.dot(ortho, basis_full.T, precision=HIGH, preferred_element_type=jnp.f...  28.8 us
    psum x1, waiting for transfers between devices, local(): gram = lax.psum(local_gram, 'fsdp')  20.4 us
  transfers between devices with their start and end apart: 4, of which 4 were waited for; matrix products, arithmetic and copies ran while one was open for 0% of the time, Pallas kernels for 0%

commit v1 on v0

--- a/solution.py
+++ b/solution.py
@@ -25,7 +25,7 @@
     chol = jnp.linalg.cholesky(gram)
     ortho = lax.linalg.triangular_solve(chol, left, left_side=False, lower=True, transpose_a=True)
     right_part = jnp.dot(buffer.T, ortho, precision=HIGH, preferred_element_type=jnp.float32)
-    right = lax.psum(right_part, ("fsdp", "replica")) / replicas
+    right = lax.psum(lax.psum(right_part, "fsdp"), "replica") / replicas
     squares = lax.psum(jnp.sum(right * right, axis=0), "tensor")
     norms = jnp.sqrt(squares + 1e-12)
     basis_full = right / norms

time: 478 us -> 528 us (1.10)
  waiting for transfers between devices: 259 us -> 308 us
    psum x1 -> x2, waiting for transfers between devices: 102 us -> 151 us  [local(): right = lax.psum(lax.psum(right_part, 'fsdp'), 'replica') / replicas]
  transfers between devices with their start and end apart: 4 -> 5, of which waited for: 4 -> 5; matrix products, arithmetic and copies ran while one was open for 0% -> 0% of each run, Pallas kernels for 0% -> 0%
where the time goes in v1:
time: 528 us; the launch traced here: 521 us
  waiting for transfers between devices  308 us (58%)
  matrix products  123 us (23%)
  other arithmetic  58.6 us (11%)
  between operations  15.7 us (3%)
  local copies, waits for them, and re-layouts  8.2 us (2%)
  blocking collectives  6.46 us (1%)
    psum x2, waiting for transfers between devices, local(): right = lax.psum(lax.psum(right_part, 'fsdp'), 'replica') / replicas  151 us
    psum x1, waiting for transfers between devices, local(): left = lax.psum(partial_value, ('tensor', 'replica')) / replicas  98.4 us
    all_gather x1, waiting for transfers between devices, local(): lax.all_gather(basis, 'fsdp', axis=1, tiled=True)  37.4 us
    another operation x6, other arithmetic, local(): chol = jnp.linalg.cholesky(gram)  34 us
    dot_general x1, matrix products, local(): jnp.dot(ortho, right.T, precision=HIGH, preferred_element_type=jnp.float32)  33.1 us
    dot_general x1, matrix products, local(): jnp.dot(buffer.T, ortho, precision=HIGH, preferred_element_type=jnp.float32)  31.3 us
    dot_general x1, matrix products, local(): jnp.dot(ortho, basis_full.T, precision=HIGH, preferred_element_type=jnp.f...  28.8 us
    psum x1, waiting for transfers between devices, local(): gram = lax.psum(local_gram, 'fsdp')  20.4 us
  transfers between devices with their start and end apart: 5, of which 5 were waited for; matrix products, arithmetic and copies ran while one was open for 0% of the time, Pallas kernels for 0%

profile of v1, /device:TPU:0, one launch (start us, length us, event | category | flops | bytes accessed | tf_op | source)
XLA Modules:
  0.0 521.1 jit_solution(12921905437739532854)
XLA Ops:
  7.2 0.7 all-gather.2.cloned.1.call-update
  7.9 37.4 %all-gather.2.cloned.1.call-done = f32[2048,256]{1,0:T(8,128)} async-done(((f32[2048,128]{1,0:T(8,128)}), f32[2048,256]{1,0:T(8,128)}) %all-gather.2.cloned.1.call-update) | async-done | bytes 2097168 | tf_op jit(solution)/shard_map/all_gather | solution.py:18
  45.3 18.8 %fusion.2 = f32[2048,256]{1,0:T(8,128)} fusion(f32[2048,256]{1,0:T(8,128)} %all-gather.2.cloned.1.call-done, f32[1,2048,2048]{2,1,0:T(8,128)} %param.4, bf16[1,2048,2048]{2,1,0:T(8,128)(2,1)} %param.3), kind=kOutput, calls=%fused_computation.5 | convolution fusion | flops 12893290496 | bytes 29360128 | tf_op jit(solution)/shard_map/dot_general | solution.py:16
  64.3 98.4 %all-reduce.6.cloned.1.call-done = f32[2048,256]{1,0:T(8,128)} async-done(((f32[2048,256]{1,0:T(8,128)}), f32[2048,256]{1,0:T(8,128)}) %all-reduce.6.cloned.1.call-update) | async-done | bytes 2097168 | tf_op jit(solution)/shard_map/psum | solution.py:22
  162.6 6.4 %fusion.19 = f32[256,256]{0,1:T(8,128)} fusion(f32[2048,256]{1,0:T(8,128)} %all-reduce.6.cloned.1.call-done), kind=kOutput, calls=%fused_computation.47 | convolution fusion | flops 1611137024 | bytes 2359296 | tf_op jit(solution)/shard_map/dot_general | solution.py:23
  169.6 1.7 broadcast_multiply_fusion
  171.4 20.4 %all-reduce.8.cloned.1.call-done = f32[256,256]{0,1:T(8,128)} async-done(((f32[256,256]{0,1:T(8,128)}), f32[256,256]{0,1:T(8,128)}) %all-reduce.8.cloned.1.call-update) | async-done | bytes 262160 | tf_op jit(solution)/shard_map/psum | solution.py:24
  191.7 1.1 copy.7
  192.8 1.0 fusion.9
  193.8 11.7 %cholesky.50 = f32[128,128]{1,0:T(8,128)S(1)} custom-call(f32[128,128]{1,0:T(8,128)S(1)} %cholesky.118), custom_call_target="Cholesky" | custom-call | tf_op jit(solution)/shard_map/jit(cholesky)/cholesky | solution.py:25
  205.6 9.8 %custom-call.14 = f32[1,128,128]{1,2,0:T(8,128)S(1)} custom-call(f32[1,128,128]{2,1,0:T(8,128)S(1)} %get-tuple-element.24), custom_call_target="InvertDiagBlocksLowerTriangular" | custom-call | tf_op jit(solution)/shard_map/jit(cholesky)/cholesky | solution.py:25
  215.9 11.7 %cholesky.105 = f32[128,128]{1,0:T(8,128)S(1)} custom-call(f32[128,128]{1,0:T(8,128)S(1)} %convolution_subtract_fusion.1), custom_call_target="Cholesky" | custom-call | tf_op jit(solution)/shard_map/jit(cholesky)/cholesky | solution.py:25
  227.6 0.6 compare_reduce_fusion
  229.7 4.2 while.1
  229.9 0.6 fusion.28
  230.5 1.4 bitcast_dynamic-update-slice_fusion.2
  231.9 0.6 fusion.28
  232.5 1.4 bitcast_dynamic-update-slice_fusion.2
  233.9 19.7 %custom-call.15 = f32[2,128,128]{1,2,0:T(8,128)S(1)} custom-call(f32[2,128,128]{2,1,0:T(8,128)S(1)} %get-tuple-element.10), custom_call_target="InvertDiagBlocksLowerTriangular" | custom-call | tf_op jit(solution)/shard_map/triangular_solve | solution.py:26
  253.5 1.1 fusion.6
  254.6 1.8 convolution_subtract_fusion
  256.5 1.1 fusion.10
  257.6 1.0 copy-done.1
  258.5 31.3 %fusion = f32[2048,256]{1,0:T(8,128)} fusion(f32[1,2048,2048]{2,1,0:T(8,128)} %param.4, bf16[1,2048,2048]{2,1,0:T(8,128)(2,1)} %param.3, f32[2048,128]{0,1:T(8,128)S(1)} %fusion.10, f32[2048,128]{0,1:T(8,128)S(1)} %fusion.6), kind=kOutput, calls=%fused_computation.3 | convolution fusion | flops 12893814784 | bytes 29360128 | tf_op jit(solution)/shard_map/dot_general | solution.py:27
  289.9 63.1 %all-reduce.10.cloned.1.call-done = f32[2048,256]{1,0:T(8,128)} async-done(((f32[2048,256]{1,0:T(8,128)}), f32[2048,256]{1,0:T(8,128)}) %all-reduce.10.cloned.1.call-update) | async-done | bytes 2097168 | tf_op jit(solution)/shard_map/psum | solution.py:28
  353.0 88.4 %all-reduce.12.cloned.1.call-done = f32[2048,256]{1,0:T(8,128)} async-done(((f32[2048,256]{1,0:T(8,128)}), f32[2048,256]{1,0:T(8,128)}) %all-reduce.12.cloned.1.call-update) | async-done | bytes 2097168 | tf_op jit(solution)/shard_map/psum | solution.py:28
  441.3 2.0 multiply_reduce_fusion
  443.4 6.5 %psum.39 = f32[256]{0:T(256)S(1)} all-reduce(f32[256]{0:T(256)S(1)} %multiply_reduce_fusion), channel_id=1, replica_groups=mesh['fsdp'=2,'tensor'=4,'replica'=4] {'tensor'}, use_global_device_ids=true, to_apply=%region_9.10 | all-reduce | flops 256 | bytes 2048 | tf_op jit(solution)/shard_map/psum | solution.py:29
  450.0 1.1 copy-done.2
  451.1 28.8 %multiply_convert_fusion = bf16[2048,2048]{1,0:T(8,128)(2,1)} fusion(f32[2048,256]{1,0:T(8,128)S(1)} %multiply_divide_fusion, f32[2048,128]{0,1:T(8,128)S(1)} %copy-done.2, f32[2048,128]{0,1:T(8,128)S(1)} %fusion.6), kind=kOutput, calls=%fused_computation.8 | convolution fusion | flops 12893814784 | bytes 12582912 | tf_op jit(solution)/shard_map/dot_general | solution.py:36
  479.9 1.0 constant_dynamic-slice_fusion.1
  480.9 33.1 %fusion.4 = f32[1,2048,2048]{2,1,0:T(8,128)} fusion(f32[1,2048,2048]{2,1,0:T(8,128)} %param.4, bf16[1,2048,2048]{2,1,0:T(8,128)(2,1)} %param.3, f32[2048,256]{1,0:T(8,128)S(1)} %copy-done, f32[2048,128]{0,1:T(8,128)S(1)} %copy-done.2, f32[2048,128]{0,1:T(8,128)S(1)} %fusion.6), kind=kOutput, calls=%fused_computation.7 | convolution fusion | flops 12902727680 | bytes 46137344 | tf_op jit(solution)/shard_map/dot_general | solution.py:32
  (27 shorter events, 1.6 us)
Async XLA Ops:
  7.2 38.2 %all-gather.2.cloned.1.call-start = ((), (), s32[]{:S(2)}) async-start(), calls=%async_computation | async-start | bytes 3145728 | tf_op jit(solution)/shard_map/all_gather | solution.py:18
  7.9 154.7 %all-reduce.6.cloned.1.call-start = ((), (), s32[]{:S(2)}) async-start(), calls=%async_computation.1 | async-start | bytes 4194304 | tf_op jit(solution)/shard_map/psum | solution.py:22
  64.2 127.5 %all-reduce.8.cloned.1.call-start = ((), (), s32[]{:S(2)}) async-start(), calls=%async_computation.2 | async-start | bytes 524288 | tf_op jit(solution)/shard_map/psum | solution.py:24
  169.1 183.9 %all-reduce.10.cloned.1.call-start = ((), (), s32[]{:S(2)}) async-start(), calls=%async_computation.3 | async-start | bytes 4194304 | tf_op jit(solution)/shard_map/psum | solution.py:28
  257.6 1.0 copy-start.1
  289.8 151.5 %all-reduce.12.cloned.1.call-start = ((), (), s32[]{:S(2)}) async-start(), calls=%async_computation.4 | async-start | bytes 4194304 | tf_op jit(solution)/shard_map/psum | solution.py:28
  441.3 8.5 %copy-start = (f32[2048,256]{1,0:T(8,128)S(1)}, f32[2048,256]{1,0:T(8,128)}, u32[]{:S(2)}) copy-start(f32[2048,256]{1,0:T(8,128)} %all-reduce.12.cloned.1.call-done) | copy-start | bytes 6291460
  449.9 1.2 copy-start.2
Sparse Core Ops, SparseCore 0:
  9.5 35.7 all-gather.1
  64.3 98.2 all-reduce.5
  169.2 22.4 all-reduce.7
  289.9 62.9 all-reduce.9
  355.2 86.1 all-reduce.11
